TPU v7x, 256 devices: a whole 4x4x8 slice. The times are simulated.
256 devices in a mesh: dp: 4 (over y), space: 64 (over x, z, core).
Axes of the slice: x: 4, y: 4, z: 8, core: 2. Of those that a mesh axis runs over, the one named last changes fastest.
Arguments:
- volume: bfloat16 [4, 128, 4, 64, 128], P('dp', 'space'), may hold values from -30 to 30
- weights_one: bfloat16 [3, 3, 3, 128, 256], replicated, may hold values from -0.109375 to 0.109375
- gain_one: float32 [256], replicated, may hold values from 0.1 to 1.9
- shift_one: float32 [256], replicated, may hold values from -3 to 3
- weights_two: bfloat16 [3, 3, 3, 8, 256], P(None, None, None, None, 'space'), may hold values from -0.4375 to 0.4375
- gain_two: float32 [256], P('space'), may hold values from 0.1 to 1.9
- shift_two: float32 [256], P('space'), may hold values from -3 to 3
- upstream: bfloat16 [4, 256, 64, 2, 32], P('dp', 'space'), may hold values from -6 to 6
Outputs:
- result: bfloat16 [4, 256, 64, 2, 32], P('dp', 'space')
- grad_weights_one: float32 [3, 3, 3, 128, 256], P(None, None, None, None, 'space')
- grad_weights_two: float32 [3, 3, 3, 8, 256], P(None, None, None, None, 'space')
All inputs are finite; a program needn't handle non-finite values.
Results may differ from a plain program's by a relative error of at most 0.0057.
Values may be sent and summed in bfloat16 or wider, within the bound.
A program may use at most 64 MiB of HBM per device.

v0:
```python
import math
import jax
import jax.numpy as jnp
from jax import lax
from jax.sharding import PartitionSpec as P

EPS = 1e-05
LAST = ("NDHWC", "DHWIO", "NDHWC")
FIRST = ("NCDHW", "DHWIO", "NCDHW")


def from_behind(value, axis, steps):
    count = lax.axis_size(axis)
    leading, last = (max(0, -steps), min(count, count - steps))
    return lax.ppermute(value, axis, [(source, source + steps) for source in range(leading, last)])


def combined_all(part, axis, combine):
    gathered = jax.tree.map(lambda a: lax.all_gather(a, axis), part)

    def take(source):
        return jax.tree.map(lambda a: lax.dynamic_index_in_dim(a, source, 0, False), gathered)

    return lax.fori_loop(
        1, lax.axis_size(axis), lambda source, state: combine(state, take(source)), take(0)
    )


def welford(left, right):
    count_a, mean_a, spread_a = left
    count_b, mean_b, spread_b = right
    merged = count_a + count_b
    delta = mean_b - mean_a
    return (
        merged,
        mean_a + delta * (count_b / merged),
        spread_a + spread_b + delta * delta * (count_a * count_b / merged),
    )


def group_filter(inputs, grads):
    return lax.conv_general_dilated(
        inputs,
        grads,
        (1, 1, 1),
        ((1, 1), (1, 1), (1, 1)),
        dimension_numbers=("CNDHW", "IODHW", "DHWNC"),
        preferred_element_type=jnp.float32,
    )


def per_device(
    volume, weights_one, gain_one, shift_one, weights_two, gain_two, shift_two, upstream
):
    planes = lax.axis_size("space")
    below = from_behind(volume[:, 1:], "space", 1)
    stacked = jnp.concatenate([below, volume], axis=1)
    pre_one = lax.conv_general_dilated(
        stacked,
        weights_one,
        (2, 2, 2),
        ((0, 0), (1, 1), (1, 1)),
        dimension_numbers=LAST,
        preferred_element_type=jnp.float32,
    )
    lead = pre_one.shape[0]
    count = float(lax.axis_size("dp") * lead * planes * pre_one.shape[2] * pre_one.shape[3])
    axes_last = (0, 1, 2, 3)
    mean_one = lax.psum(jnp.sum(pre_one, axis=axes_last), ("dp", "space")) / count
    spread_one = lax.psum(jnp.sum(jnp.square(pre_one - mean_one), axis=axes_last), ("dp", "space"))
    var_one = spread_one / count
    inv_one = lax.rsqrt(var_one + EPS)
    norm_one = (pre_one - mean_one) * inv_one
    act_in = norm_one * gain_one + shift_one
    activated = jax.nn.silu(act_in).astype(jnp.bfloat16)
    act_first = jnp.transpose(activated, (0, 4, 1, 2, 3))
    own_width = weights_two.shape[4]
    group_width = weights_two.shape[3]
    window = max(own_width, group_width)
    replicas = window // own_width
    channels = act_first.shape[1]
    tail = act_first.shape[2:]
    parts = act_first.reshape((lead, channels // window, 1, window) + tail)
    copies = jnp.broadcast_to(parts, (lead, channels // window, replicas, window) + tail)
    outgoing = copies.reshape((lead, planes * window) + tail)
    inputs = lax.all_to_all(outgoing, "space", split_axis=1, concat_axis=2, tiled=True)
    groups_here = window // group_width
    per_group = own_width // groups_here
    padding_one = ((1, 1), (1, 1), (1, 1))
    pre_two = lax.conv_general_dilated(
        inputs,
        weights_two,
        (1, 1, 1),
        padding_one,
        dimension_numbers=FIRST,
        feature_group_count=groups_here,
        preferred_element_type=jnp.float32,
    )
    axes_first = (0, 2, 3, 4)
    local_mean_two = jnp.mean(pre_two, axis=axes_first, keepdims=True)
    local_spread_two = jnp.sum(jnp.square(pre_two - local_mean_two), axis=axes_first, keepdims=True)
    local_count_two = float(pre_two.size // pre_two.shape[1])
    merged_two, mean_two, spread_two = combined_all(
        (jnp.full((1, 1, 1, 1, 1), local_count_two, jnp.float32), local_mean_two, local_spread_two),
        "dp",
        welford,
    )
    inv_two = lax.rsqrt(spread_two / merged_two + EPS)
    norm_two = (pre_two - mean_two) * inv_two
    gain_col = gain_two.reshape((1, -1, 1, 1, 1))
    shift_col = shift_two.reshape((1, -1, 1, 1, 1))
    result = (norm_two * gain_col + shift_col).astype(jnp.bfloat16)
    grad_norm_two = upstream.astype(jnp.float32) * gain_col * (1.0 / math.sqrt(count))
    first_sum, second_sum = lax.psum(
        (
            jnp.sum(grad_norm_two, axis=axes_first, keepdims=True),
            jnp.sum(grad_norm_two * norm_two, axis=axes_first, keepdims=True),
        ),
        "dp",
    )
    grad_pre_two = (
        inv_two * (grad_norm_two - first_sum / count - norm_two * (second_sum / count))
    ).astype(jnp.bfloat16)
    grouped_inputs = inputs.reshape((lead, groups_here, group_width) + inputs.shape[2:])
    grouped_grads = grad_pre_two.reshape((lead, groups_here, per_group) + grad_pre_two.shape[2:])
    pieces = jax.vmap(group_filter, in_axes=(1, 1))(grouped_inputs, grouped_grads)
    local_two = jnp.transpose(pieces, (1, 2, 3, 4, 0, 5)).reshape((3, 3, 3, group_width, own_width))
    grad_weights_two = lax.psum(local_two, "dp")
    flipped = weights_two[::-1, ::-1, ::-1]
    turned = (
        flipped.reshape((3, 3, 3, group_width, groups_here, per_group))
        .transpose((0, 1, 2, 5, 4, 3))
        .reshape((3, 3, 3, per_group, window))
    )
    partial_grad = lax.conv_general_dilated(
        grad_pre_two,
        turned,
        (1, 1, 1),
        padding_one,
        dimension_numbers=FIRST,
        feature_group_count=groups_here,
        preferred_element_type=jnp.float32,
    )
    arrived = lax.all_to_all(partial_grad, "space", split_axis=2, concat_axis=1, tiled=True)
    grad_act = jnp.sum(
        arrived.reshape((lead, channels // window, replicas, window) + arrived.shape[2:]), axis=2
    ).reshape((lead, channels) + arrived.shape[2:])
    grad_last = jnp.transpose(grad_act, (0, 2, 3, 4, 1))
    sigma = jax.nn.sigmoid(act_in)
    grad_norm_one = grad_last * (sigma * (1.0 + act_in * (1.0 - sigma))) * gain_one
    third_sum, fourth_sum = lax.psum(
        (jnp.sum(grad_norm_one, axis=axes_last), jnp.sum(grad_norm_one * norm_one, axis=axes_last)),
        ("dp", "space"),
    )
    grad_pre_one = (
        inv_one * (grad_norm_one - third_sum / count - norm_one * (fourth_sum / count))
    ).astype(jnp.bfloat16)
    local_one = lax.conv_general_dilated(
        stacked,
        grad_pre_one,
        (1, 1, 1),
        ((0, 0), (1, 0), (1, 0)),
        rhs_dilation=(2, 2, 2),
        dimension_numbers=("CDHWN", "IDHWO", "DHWNC"),
        preferred_element_type=jnp.float32,
    )
    summed = lax.psum(local_one, "dp")
    grad_weights_one = lax.psum_scatter(summed, "space", scatter_dimension=4, tiled=True)
    return (result, grad_weights_one, grad_weights_two)


def solution(mesh):
    return jax.shard_map(
        per_device,
        mesh=mesh,
        in_specs=(
            P("dp", "space", None, None, None),
            P(),
            P(),
            P(),
            P(None, None, None, None, "space"),
            P("space"),
            P("space"),
            P("dp", "space", None, None, None),
        ),
        out_specs=(
            P("dp", "space", None, None, None),
            P(None, None, None, None, "space"),
            P(None, None, None, None, "space"),
        ),
        check_vma=False,
    )
```

profile of v0, /device:TPU:2, one launch (start us, length us, event | category | flops | bytes accessed | tf_op | source)
XLA Modules:
  0.0 559.2 jit_solution(1003987523249396105)
XLA Ops:
  7.2 1.0 slice.21
  8.3 1.9 collective-permute-start
  10.2 7.9 %collective-permute-done = bf16[1,1,4,64,128]{4,0,3,2,1:T(2,128)(2,1)S(1)} collective-permute-done((bf16[1,1,4,64,128]{4,0,3,2,1:T(2,128)(2,1)S(1)}, bf16[1,1,4,64,128]{4,0,3,2,1:T(2,128)(2,1)S(1)}, u32[]{:S(2)}, u32[]{:S(2)}) %collective-permute-start) | collective-permute-done | bytes 65568 | tf_op jit(solution)/shard_map/ppermute | solution.py:15
  18.2 1.1 constant_dynamic-update-slice_fusion
  19.4 0.7 copy-done.1
  21.0 74.9 %psum.56 = f32[256]{0:T(256)S(1)} all-reduce(f32[256]{0:T(256)S(1)} %get-tuple-element.289), channel_id=1, replica_groups=mesh['dp'=4,'space'=64] {'dp','space'}, use_global_device_ids=true, to_apply=%region_1.0 | all-reduce | flops 256 | bytes 2048 | tf_op jit(solution)/shard_map/psum | solution.py:69
  95.9 74.4 %psum.57 = f32[256]{0:T(256)S(1)} all-reduce(f32[256]{0:T(256)S(1)} %select_reduce_fusion.2), channel_id=1, replica_groups=mesh['dp'=4,'space'=64] {'dp','space'}, use_global_device_ids=true, to_apply=%region_3.0 | all-reduce | flops 256 | bytes 2048 | tf_op jit(solution)/shard_map/psum | solution.py:70
  170.5 0.4 copy-done.9
  171.3 0.8 reshape.180
  172.2 8.1 %all-to-all-start = ((bf16[64,2,256]{2,1,0:T(2,128)(2,1)}), bf16[64,2,256]{2,1,0:T(2,128)(2,1)S(1)}, u32[]{:S(2)}, u32[]{:S(2)}) async-start(bf16[64,2,256]{2,1,0:T(2,128)(2,1)} %reshape.180), calls=%async_computation | async-start | bytes 131072 | tf_op jit(solution)/shard_map/all_to_all | solution.py:86
  180.3 0.6 rev.3
  180.9 0.6 dynamic-slice
  182.2 0.8 dynamic-update-slice
  183.0 6.0 %all-to-all-done = bf16[64,2,256]{2,1,0:T(2,128)(2,1)S(1)} async-done(((bf16[64,2,256]{2,1,0:T(2,128)(2,1)}), bf16[64,2,256]{2,1,0:T(2,128)(2,1)S(1)}, u32[]{:S(2)}, u32[]{:S(2)}) %all-to-all-start) | async-done | bytes 65568 | tf_op jit(solution)/shard_map/all_to_all | solution.py:86
  189.5 0.7 pad.2.clone
  190.2 2.1 copy.207
  192.5 5.6 fusion.8
  198.1 1.7 copy.208
  200.5 8.6 %all-reduce.7 = (f32[4]{0:T(128)S(1)}, f32[16]{0:T(128)S(1)}, f32[16]{0:T(128)S(1)}) all-reduce(f32[4]{0:T(128)S(1)} %dynamic-update-slice, f32[16]{0:T(128)S(1)} %get-tuple-element.288, f32[16]{0:T(128)S(1)} %dynamic-update-slice.2), channel_id=1, replica_groups=mesh['dp'=4,'space'=64] {'dp'}, use_global_device_ids=true, to_apply=%add | all-reduce | flops 36 | bytes 288
  209.8 13.6 %while.19 = (s32[]{:T(128)}, f32[1,1,1,1,1]{4,3,2,1,0:T(1,128)}, f32[1,4,1,1,1]{1,4,3,2,0:T(1,128)S(1)}, f32[1,4,1,1,1]{1,4,3,2,0:T(1,128)S(1)}, f32[4,1,1,1,1,1...) while((s32[]{:T(128)}, f32[1,1,1,1,1]{4,3,2,1,0:T(1,128)}, ...), condition=%wide.region_7.8_spmd, body=%wide.region_6.7_spmd.sunk | while | flops 37 | bytes 303 | solution.py:24
  209.8 0.6 constant_dynamic-slice_fusion.5
  214.4 0.6 constant_dynamic-slice_fusion.5
  218.9 0.6 constant_dynamic-slice_fusion.5
  223.5 0.7 rsqrt_bitcast_fusion
  224.1 0.8 add_convert_fusion
  225.2 9.4 %all-reduce.6 = (f32[1,4,1,1,1]{1,4,3,2,0:T(1,128)S(1)}, f32[1,4,1,1,1]{1,4,3,2,0:T(1,128)S(1)}) all-reduce(f32[1,4,1,1,1]{1,4,3,2,0:T(1,128)S(1)} %bitcast.177, f32[1,4,1,1,1]{1,4,3,2,0:T(1,128)S(1)} %bitcast.176), channel_id=1, replica_groups=mesh['dp'=4,'space'=64] {'dp'}, use_global_device_ids=true, to_apply=%region_11.12 | all-reduce | flops 8 | bytes 64 | tf_op jit(solution)/shard_map/psum | solution.py:114
  235.5 6.9 %convolution_select_fusion = f32[64,2,8,5,8]{4,2,3,1,0:T(8,128)} fusion(pred[8,5]{0,1:T(8,128)(4,1)S(1)} %copy-done.7, bf16[4,64,2,1,7,2]{4,0,5,2,1,3:T(4,128)(2,1)S(1)} %slice.28, bf16[4,64,2,1,8,5]{4,0,5,2,1,3:T(4,128)(2,1)S(1)} %copy.218, bf16[3,3,3,8,4]{3,4,2,1,0:T(4,128)(2,1)S(1)} %copy-done.6), kind=kOutput, calls=%fused_computation.19 | convolution fusion | flops 6049792 | bytes 220904 | tf_op jit(solution)/shard_map/conv_general_dilated | solution.py:135
  242.5 2.6 copy.219
  245.4 0.9 reshape.182
  246.4 5.5 all-to-all-start.1
  252.2 0.8 copy.241
  253.0 8.2 %all-to-all-done.1 = f32[64,1,512]{2,1,0:T(1,128)S(1)} async-done(((f32[64,1,512]{2,1,0:T(1,128)}), f32[64,1,512]{2,1,0:T(1,128)S(1)}, u32[]{:S(2)}, u32[]{:S(2)}) %all-to-all-start.1) | async-done | bytes 131104 | tf_op jit(solution)/shard_map/all_to_all | solution.py:144
  261.2 0.5 broadcast.186
  261.7 0.9 reduce.1
  262.9 0.7 reduce_sum.87
  263.6 1.3 fusion.51
  264.9 73.3 %all-reduce.4 = (f32[256]{0:T(256)S(1)}, f32[256]{0:T(256)S(1)}) all-reduce(f32[256]{0:T(256)S(1)} %get-tuple-element.252, f32[256]{0:T(256)S(1)} %get-tuple-element.251), channel_id=1, replica_groups=mesh['dp'=4,'space'=64] {'dp','space'}, use_global_device_ids=true, to_apply=%region_16.17 | all-reduce | flops 512 | bytes 4096 | tf_op jit(solution)/shard_map/psum | solution.py:151
  338.4 0.8 fusion.31
  339.4 2.8 fusion.53
  342.3 0.6 copy-done.13
  342.9 0.6 dynamic-slice.3
  344.1 3.5 copy.231
  347.7 0.6 copy.232
  348.3 3.4 copy.230
  351.7 29.6 %fusion.54 = f32[3,3,3,8,4]{3,4,2,1,0:T(4,128)S(1)} fusion(bf16[1,8,64,2,32]{1,0,4,3,2:T(2,128)(2,1)} %copy.230, bf16[1,4,64,2,32]{1,0,4,3,2:T(2,128)(2,1)} %copy.231), kind=kOutput, calls=%fused_computation.97 | convolution fusion | flops 4572160 | bytes 101760 | tf_op jit(solution)/shard_map/vmap()/conv_general_dilated | solution.py:42
  381.3 151.0 %all-reduce.10.cloned.1.call-done = f32[3,3,3,128,256]{3,4,2,1,0:T(8,128)} async-done(((f32[3,3,3,128,256]{3,4,2,1,0:T(8,128)}), f32[3,3,3,128,256]{3,4,2,1,0:T(8,128)}) %all-reduce.10.cloned.1.call-update) | async-done | bytes 3538960
  532.3 0.9 constant_dynamic-slice_fusion.3
  533.3 18.7 %all-reduce.5 = (f32[3,3,3,128,4]{3,4,2,1,0:T(4,128)}, f32[3,3,3,8,4]{3,4,2,1,0:T(4,128)}) all-reduce(f32[3,3,3,128,4]{3,4,2,1,0:T(4,128)S(1)} %constant_dynamic-slice_fusion.3, f32[3,3,3,8,4]{3,4,2,1,0:T(4,128)S(1)} %fusion.54), channel_id=1, replica_groups=mesh['dp'=4,'space'=64] {'dp'}, use_global_device_ids=true, to_apply=%region_17.18 | all-reduce | flops 14688 | bytes 117504 | tf_op jit(solution)/shard_map/psum | solution.py:167
  (91 shorter events, 5.7 us)
Async XLA Ops:
  7.2 13.3 %copy-start = (bf16[3,3,3,128,256]{4,3,2,1,0:T(8,128)(2,1)S(1)}, bf16[3,3,3,128,256]{4,3,2,1,0:T(8,128)(2,1)}, u32[]{:S(2)}) copy-start(bf16[3,3,3,128,256]{4,3,2,1,0:T(8,128)(2,1)} %param.11) | copy-start | bytes 5308420
  7.2 13.3 %copy-start.7 = (pred[8,5]{0,1:T(8,128)(4,1)S(1)}, pred[8,5]{0,1:T(8,128)(4,1)}, u32[]{:S(2)}) copy-start(pred[8,5]{0,1:T(8,128)(4,1)} %constant.99) | copy-start | bytes 124
  8.3 9.8 %collective-permute-start = (bf16[1,1,4,64,128]{4,0,3,2,1:T(2,128)(2,1)S(1)}, bf16[1,1,4,64,128]{4,0,3,2,1:T(2,128)(2,1)S(1)}, u32[]{:S(2)}, u32[]{:S(2)}) collective-permute-start(bf16[1,1,4,64,128]{4,0,3,2,1:T(2,128)(2,1)S(1)} %copy.254), channel_id=1, source_target_pairs={{0,1},{1,2},{2,3},{3,4},{4,5},{5,6},{6,7},{7,8},{8,9},{9,10},{10,1... | collective-permute-start | bytes 196616 | tf_op jit(solution)/shard_map/ppermute | solution.py:15
  19.4 0.7 copy-start.1
  20.1 150.2 %copy-start.8 = (f32[256]{0:T(256)S(1)}, f32[256]{0:T(256)}, u32[]{:S(2)}) copy-start(f32[256]{0:T(256)} %param.12) | copy-start | bytes 3076
  20.1 150.2 %copy-start.11 = (f32[256]{0:T(256)S(1)}, f32[256]{0:T(256)}, u32[]{:S(2)}) copy-start(f32[256]{0:T(256)} %param.13) | copy-start | bytes 3076
  20.5 159.8 %copy-start.5 = (bf16[3,3,3,8,4]{3,4,2,1,0:T(4,128)(2,1)S(1)}, bf16[3,3,3,8,4]{3,4,2,1,0:T(4,128)(2,1)}, u32[]{:S(2)}) copy-start(bf16[3,3,3,8,4]{3,4,2,1,0:T(4,128)(2,1)} %param.14) | copy-start | bytes 5188
  20.5 160.4 %copy-start.14 = (u32[256]{0:T(256)S(1)}, u32[256]{0:T(256)}, u32[]{:S(2)}) copy-start(u32[256]{0:T(256)} %constant.108) | copy-start | bytes 3076
  170.3 0.6 copy-start.9
  172.2 16.9 %all-to-all-start = ((bf16[64,2,256]{2,1,0:T(2,128)(2,1)}), bf16[64,2,256]{2,1,0:T(2,128)(2,1)S(1)}, u32[]{:S(2)}, u32[]{:S(2)}) async-start(bf16[64,2,256]{2,1,0:T(2,128)(2,1)} %reshape.180), calls=%async_computation | async-start | bytes 131072 | tf_op jit(solution)/shard_map/all_to_all | solution.py:86
  198.1 26.0 %copy-start.10 = (f32[4]{0:T(128)S(1)}, f32[4]{0:T(128)}, u32[]{:S(2)}) copy-start(f32[4]{0:T(128)} %param.15) | copy-start | bytes 52
  198.1 26.1 %copy-start.12 = (f32[4]{0:T(128)S(1)}, f32[4]{0:T(128)}, u32[]{:S(2)}) copy-start(f32[4]{0:T(128)} %param.16) | copy-start | bytes 52
  198.1 26.9 %copy-start.4 = (bf16[1,4,64,2,32]{2,4,3,1,0:T(8,128)(2,1)S(1)}, bf16[1,4,64,2,32]{2,4,3,1,0:T(8,128)(2,1)}, u32[]{:S(2)}) copy-start(bf16[1,4,64,2,32]{2,4,3,1,0:T(8,128)(2,1)} %param.17) | copy-start | bytes 98308
  199.8 35.7 %copy-start.6 = (bf16[3,3,3,8,4]{3,4,2,1,0:T(4,128)(2,1)S(1)}, bf16[3,3,3,8,4]{3,4,2,1,0:T(4,128)(2,1)}, u32[]{:S(2)}) copy-start(bf16[3,3,3,8,4]{3,4,2,1,0:T(4,128)(2,1)} %rev.3) | copy-start | bytes 5188
  246.4 14.9 %all-to-all-start.1 = ((f32[64,1,512]{2,1,0:T(1,128)}), f32[64,1,512]{2,1,0:T(1,128)S(1)}, u32[]{:S(2)}, u32[]{:S(2)}) async-start(f32[64,1,512]{2,1,0:T(1,128)} %reshape.182), calls=%async_computation.1 | async-start | bytes 262144 | tf_op jit(solution)/shard_map/all_to_all | solution.py:144
  251.8 280.5 %all-reduce.10.cloned.1.call-start = ((), (), s32[]{:S(2)}) async-start(), calls=%async_computation.2 | async-start | bytes 7077888
  262.7 76.7 %copy-start.2 = (bf16[1,3,4,64,128]{4,0,3,2,1:T(2,128)(2,1)S(1)}, bf16[1,3,4,64,128]{4,0,3,2,1:T(2,128)(2,1)}, u32[]{:S(2)}) copy-start(bf16[1,3,4,64,128]{4,0,3,2,1:T(2,128)(2,1)} %copy-done.1) | copy-start | bytes 589828
  342.2 0.7 copy-start.13
  342.2 5.4 copy-start.3
Sparse Core Ops, SparseCore 0:
  342.4 189.9 all-reduce.9
where the time goes:
time: 568 us; the launch traced here: 559 us
  blocking collectives  259 us (46%)
  waiting for transfers between devices  173 us (30%)
  matrix products  45.4 us (8%)
  local copies, waits for them, and re-layouts  31 us (5%)
  between operations  16.8 us (3%)
  starting transfers between devices  15.5 us (3%)
  loops' own time  11.6 us (2%)
  other arithmetic  6.47 us (1%)
    unnamed x2, waiting for transfers between devices  151 us
    psum x1, blocking collectives, per_device(): lax.psum(jnp.sum(pre_one, axis=axes_last), ('dp', 'space')) / count  74.9 us
    psum x1, blocking collectives, per_device(): lax.psum(jnp.sum(jnp.square(pre_one - mean_one), axis=axes_last), ('dp',...  74.4 us
    psum x1, blocking collectives, per_device(): lax.psum((jnp.sum(grad_norm_one, axis=axes_last), jnp.sum(grad_norm_one *...  73.3 us
    conv_general_dilated x1, matrix products, group_filter(): lax.conv_general_dilated(inputs, grads, (1, 1, 1), ((1, 1), (1, 1), (1, 1...  29.6 us
    psum x1, blocking collectives, per_device(): summed = lax.psum(local_one, 'dp')  18.7 us
    another operation x1, loops' own time, combined_all(): lax.fori_loop(1, lax.axis_size(axis), lambda source, state: combine(state...  11.6 us
  transfers between devices with their start and end apart: 4, of which 4 were waited for; matrix products, arithmetic and copies ran while one was open for 7% of the time, Pallas kernels for 0%

commit v1 on v0

--- a/solution.py
+++ b/solution.py
@@ -67,7 +67,10 @@
     count = float(lax.axis_size("dp") * lead * planes * pre_one.shape[2] * pre_one.shape[3])
     axes_last = (0, 1, 2, 3)
     mean_one = lax.psum(jnp.sum(pre_one, axis=axes_last), ("dp", "space")) / count
-    spread_one = lax.psum(jnp.sum(jnp.square(pre_one - mean_one), axis=axes_last), ("dp", "space"))
+    spread_one = jnp.sum(
+        lax.all_gather(jnp.sum(jnp.square(pre_one - mean_one), axis=axes_last), ("dp", "space")),
+        axis=0,
+    )
     var_one = spread_one / count
     inv_one = lax.rsqrt(var_one + EPS)
     norm_one = (pre_one - mean_one) * inv_one

time: 568 us -> 551 us (0.970)
  blocking collectives: 259 us -> 244 us
    psum x1 -> x0, blocking collectives: 74.4 us -> none  [per_device(): lax.psum(jnp.sum(jnp.square(pre_one - mean_one), axis=axes_last), ('dp',...]
    all_gather x0 -> x1, blocking collectives: none -> 59.6 us  [per_device(): lax.all_gather(jnp.sum(jnp.square(pre_one - mean_one), axis=axes_last), (...]
  transfers between devices with their start and end apart: 4 -> 4, of which waited for: 4 -> 4; matrix products, arithmetic and copies ran while one was open for 7% -> 8% of each run, Pallas kernels for 0% -> 0%
where the time goes in v1:
time: 551 us; the launch traced here: 542 us
  blocking collectives  244 us (44%)
  waiting for transfers between devices  173 us (31%)
  matrix products  45.3 us (8%)
  local copies, waits for them, and re-layouts  28.8 us (5%)
  between operations  16.6 us (3%)
  starting transfers between devices  16 us (3%)
  loops' own time  10.6 us (2%)
  other arithmetic  6.7 us (1%)
    unnamed x2, waiting for transfers between devices  151 us
    psum x1, blocking collectives, per_device(): lax.psum(jnp.sum(pre_one, axis=axes_last), ('dp', 'space')) / count  74.9 us
    psum x1, blocking collectives, per_device(): lax.psum((jnp.sum(grad_norm_one, axis=axes_last), jnp.sum(grad_norm_one *...  73.6 us
    all_gather x1, blocking collectives, per_device(): lax.all_gather(jnp.sum(jnp.square(pre_one - mean_one), axis=axes_last), (...  59.6 us
    conv_general_dilated x1, matrix products, group_filter(): lax.conv_general_dilated(inputs, grads, (1, 1, 1), ((1, 1), (1, 1), (1, 1...  29.6 us
    psum x1, blocking collectives, per_device(): summed = lax.psum(local_one, 'dp')  18.7 us
  transfers between devices with their start and end apart: 4, of which 4 were waited for; matrix products, arithmetic and copies ran while one was open for 8% of the time, Pallas kernels for 0%

profile of v1, /device:TPU:2, one launch (start us, length us, event | category | flops | bytes accessed | tf_op | source)
XLA Modules:
  0.0 542.0 jit_solution(12251253862458468227)
XLA Ops:
  7.2 1.0 slice.21
  8.3 1.9 collective-permute-start
  10.2 7.9 %collective-permute-done = bf16[1,1,4,64,128]{4,0,3,2,1:T(2,128)(2,1)S(1)} collective-permute-done((bf16[1,1,4,64,128]{4,0,3,2,1:T(2,128)(2,1)S(1)}, bf16[1,1,4,64,128]{4,0,3,2,1:T(2,128)(2,1)S(1)}, u32[]{:S(2)}, u32[]{:S(2)}) %collective-permute-start) | collective-permute-done | bytes 65568 | tf_op jit(solution)/shard_map/ppermute | solution.py:15
  18.2 1.1 constant_dynamic-update-slice_fusion
  19.4 0.7 copy-done.1
  20.5 0.4 select_reduce_fusion.3
  21.0 74.9 %psum.49 = f32[256]{0:T(256)S(1)} all-reduce(f32[256]{0:T(256)S(1)} %get-tuple-element.289), channel_id=1, replica_groups=mesh['dp'=4,'space'=64] {'dp','space'}, use_global_device_ids=true, to_apply=%region_1.0 | all-reduce | flops 256 | bytes 2048 | tf_op jit(solution)/shard_map/psum | solution.py:69
  96.0 59.6 %all-gather.3 = f32[256,1,256]{2,1,0:T(1,128)S(1)} all-gather(f32[1,1,256]{2,1,0:T(1,128)S(1)} %bitcast.177), channel_id=2, replica_groups=mesh['dp'=4,'space'=64] {'dp','space'}, dimensions={0}, use_global_device_ids=true | all-gather | bytes 263168 | tf_op jit(solution)/shard_map/all_gather | solution.py:71
  155.9 0.7 add_multiply_fusion
  157.1 0.8 reshape.188
  157.9 8.5 %all-to-all-start = ((bf16[64,2,256]{2,1,0:T(2,128)(2,1)}), bf16[64,2,256]{2,1,0:T(2,128)(2,1)S(1)}, u32[]{:S(2)}, u32[]{:S(2)}) async-start(bf16[64,2,256]{2,1,0:T(2,128)(2,1)} %reshape.188), calls=%async_computation | async-start | bytes 131072 | tf_op jit(solution)/shard_map/all_to_all | solution.py:89
  166.5 0.6 rev.3
  167.1 0.6 dynamic-slice
  168.3 0.7 dynamic-update-slice
  169.1 6.2 %all-to-all-done = bf16[64,2,256]{2,1,0:T(2,128)(2,1)S(1)} async-done(((bf16[64,2,256]{2,1,0:T(2,128)(2,1)}), bf16[64,2,256]{2,1,0:T(2,128)(2,1)S(1)}, u32[]{:S(2)}, u32[]{:S(2)}) %all-to-all-start) | async-done | bytes 65568 | tf_op jit(solution)/shard_map/all_to_all | solution.py:89
  175.8 1.0 copy.207
  177.0 5.6 %fusion.8 = f32[64,2,8,5,4]{2,4,3,1,0:T(4,128)} fusion(bf16[3,3,3,8,4]{3,4,2,1,0:T(4,128)(2,1)S(1)} %copy-done.8, bf16[8,64,2,1,7,2]{4,0,5,2,1,3:T(8,128)(2,1)S(1)} %slice.24, bf16[8,64,2,1,8,5]{4,0,5,2,1,3:T(8,128)(2,1)S(1)} %copy.207), kind=kOutput, calls=%fused_computation.13 | convolution fusion | flops 6180864 | bytes 194240 | tf_op jit(solution)/shard_map/conv_general_dilated | solution.py:93
  182.6 1.7 copy.208
  185.0 9.7 %all-reduce.7 = (f32[4]{0:T(128)S(1)}, f32[16]{0:T(128)S(1)}, f32[16]{0:T(128)S(1)}) all-reduce(f32[4]{0:T(128)S(1)} %dynamic-update-slice, f32[16]{0:T(128)S(1)} %get-tuple-element.288, f32[16]{0:T(128)S(1)} %dynamic-update-slice.2), channel_id=1, replica_groups=mesh['dp'=4,'space'=64] {'dp'}, use_global_device_ids=true, to_apply=%add | all-reduce | flops 36 | bytes 288
  195.4 12.4 %while.19 = (s32[]{:T(128)}, f32[1,1,1,1,1]{4,3,2,1,0:T(1,128)}, f32[1,4,1,1,1]{1,4,3,2,0:T(1,128)S(1)}, f32[1,4,1,1,1]{1,4,3,2,0:T(1,128)S(1)}, f32[4,1,1,1,1,1...) while((s32[]{:T(128)}, f32[1,1,1,1,1]{4,3,2,1,0:T(1,128)}, ...), condition=%wide.region_7.8_spmd, body=%wide.region_6.7_spmd.sunk | while | flops 37 | bytes 303 | solution.py:24
  195.4 0.6 constant_dynamic-slice_fusion.5
  199.5 0.6 constant_dynamic-slice_fusion.5
  203.7 0.6 constant_dynamic-slice_fusion.5
  207.8 0.7 rsqrt_bitcast_fusion
  208.5 0.8 add_convert_fusion
  209.6 8.0 %all-reduce.6 = (f32[1,4,1,1,1]{1,4,3,2,0:T(1,128)S(1)}, f32[1,4,1,1,1]{1,4,3,2,0:T(1,128)S(1)}) all-reduce(f32[1,4,1,1,1]{1,4,3,2,0:T(1,128)S(1)} %bitcast.179, f32[1,4,1,1,1]{1,4,3,2,0:T(1,128)S(1)} %bitcast.178), channel_id=1, replica_groups=mesh['dp'=4,'space'=64] {'dp'}, use_global_device_ids=true, to_apply=%region_11.12 | all-reduce | flops 8 | bytes 64 | tf_op jit(solution)/shard_map/psum | solution.py:117
  217.9 0.4 copy.218
  218.5 6.9 %convolution_select_fusion = f32[64,2,8,5,8]{4,2,3,1,0:T(8,128)} fusion(pred[8,5]{0,1:T(8,128)(4,1)S(1)} %copy-done.10, bf16[4,64,2,1,7,2]{4,0,5,2,1,3:T(4,128)(2,1)S(1)} %slice.28, bf16[4,64,2,1,8,5]{4,0,5,2,1,3:T(4,128)(2,1)S(1)} %copy.218, bf16[3,3,3,8,4]{3,4,2,1,0:T(4,128)(2,1)S(1)} %copy-done.9), kind=kOutput, calls=%fused_computation.19 | convolution fusion | flops 6049792 | bytes 220904 | tf_op jit(solution)/shard_map/conv_general_dilated | solution.py:138
  225.4 2.7 copy.219
  228.4 0.9 reshape.190
  229.3 5.5 %all-to-all-start.1 = ((f32[64,1,512]{2,1,0:T(1,128)}), f32[64,1,512]{2,1,0:T(1,128)S(1)}, u32[]{:S(2)}, u32[]{:S(2)}) async-start(f32[64,1,512]{2,1,0:T(1,128)} %reshape.190), calls=%async_computation.1 | async-start | bytes 262144 | tf_op jit(solution)/shard_map/all_to_all | solution.py:147
  235.2 0.8 copy.241
  236.0 8.2 %all-to-all-done.1 = f32[64,1,512]{2,1,0:T(1,128)S(1)} async-done(((f32[64,1,512]{2,1,0:T(1,128)}), f32[64,1,512]{2,1,0:T(1,128)S(1)}, u32[]{:S(2)}, u32[]{:S(2)}) %all-to-all-start.1) | async-done | bytes 131104 | tf_op jit(solution)/shard_map/all_to_all | solution.py:147
  244.2 0.5 broadcast.193
  244.7 0.9 reduce.2
  245.9 0.7 reduce_sum.97
  246.6 1.3 fusion.51
  247.9 73.6 %all-reduce.4 = (f32[256]{0:T(256)S(1)}, f32[256]{0:T(256)S(1)}) all-reduce(f32[256]{0:T(256)S(1)} %get-tuple-element.252, f32[256]{0:T(256)S(1)} %get-tuple-element.251), channel_id=1, replica_groups=mesh['dp'=4,'space'=64] {'dp','space'}, use_global_device_ids=true, to_apply=%region_16.17 | all-reduce | flops 512 | bytes 4096 | tf_op jit(solution)/shard_map/psum | solution.py:154
  322.0 2.8 fusion.53
  324.9 0.6 copy-done.15
  325.6 0.6 dynamic-slice.3
  326.8 3.5 copy.231
  330.3 0.6 copy.232
  331.0 3.6 copy.230
  334.6 29.6 %fusion.54 = f32[3,3,3,8,4]{3,4,2,1,0:T(4,128)S(1)} fusion(bf16[1,8,64,2,32]{1,0,4,3,2:T(2,128)(2,1)} %copy.230, bf16[1,4,64,2,32]{1,0,4,3,2:T(2,128)(2,1)} %copy.231), kind=kOutput, calls=%fused_computation.97 | convolution fusion | flops 4572160 | bytes 101760 | tf_op jit(solution)/shard_map/vmap()/conv_general_dilated | solution.py:42
  364.2 151.2 %all-reduce.10.cloned.1.call-done = f32[3,3,3,128,256]{3,4,2,1,0:T(8,128)} async-done(((f32[3,3,3,128,256]{3,4,2,1,0:T(8,128)}), f32[3,3,3,128,256]{3,4,2,1,0:T(8,128)}) %all-reduce.10.cloned.1.call-update) | async-done | bytes 3538960
  515.3 0.9 constant_dynamic-slice_fusion.3
  516.2 18.7 %all-reduce.5 = (f32[3,3,3,128,4]{3,4,2,1,0:T(4,128)}, f32[3,3,3,8,4]{3,4,2,1,0:T(4,128)}) all-reduce(f32[3,3,3,128,4]{3,4,2,1,0:T(4,128)S(1)} %constant_dynamic-slice_fusion.3, f32[3,3,3,8,4]{3,4,2,1,0:T(4,128)S(1)} %fusion.54), channel_id=1, replica_groups=mesh['dp'=4,'space'=64] {'dp'}, use_global_device_ids=true, to_apply=%region_17.18 | all-reduce | flops 14688 | bytes 117504 | tf_op jit(solution)/shard_map/psum | solution.py:170
  (96 shorter events, 5.3 us)
Async XLA Ops:
  7.2 13.3 %copy-start = (bf16[3,3,3,128,256]{4,3,2,1,0:T(8,128)(2,1)S(1)}, bf16[3,3,3,128,256]{4,3,2,1,0:T(8,128)(2,1)}, u32[]{:S(2)}) copy-start(bf16[3,3,3,128,256]{4,3,2,1,0:T(8,128)(2,1)} %param.11) | copy-start | bytes 5308420
  7.2 13.3 %copy-start.10 = (pred[8,5]{0,1:T(8,128)(4,1)S(1)}, pred[8,5]{0,1:T(8,128)(4,1)}, u32[]{:S(2)}) copy-start(pred[8,5]{0,1:T(8,128)(4,1)} %constant.99) | copy-start | bytes 124
  8.3 9.8 %collective-permute-start = (bf16[1,1,4,64,128]{4,0,3,2,1:T(2,128)(2,1)S(1)}, bf16[1,1,4,64,128]{4,0,3,2,1:T(2,128)(2,1)S(1)}, u32[]{:S(2)}, u32[]{:S(2)}) collective-permute-start(bf16[1,1,4,64,128]{4,0,3,2,1:T(2,128)(2,1)S(1)} %copy.254), channel_id=1, source_target_pairs={{0,1},{1,2},{2,3},{3,4},{4,5},{5,6},{6,7},{7,8},{8,9},{9,10},{10,1... | collective-permute-start | bytes 196616 | tf_op jit(solution)/shard_map/ppermute | solution.py:15
  19.4 0.7 copy-start.1
  20.2 135.7 %copy-start.11 = (f32[256]{0:T(256)S(1)}, f32[256]{0:T(256)}, u32[]{:S(2)}) copy-start(f32[256]{0:T(256)} %param.12) | copy-start | bytes 3076
  20.2 135.7 %copy-start.13 = (f32[256]{0:T(256)S(1)}, f32[256]{0:T(256)}, u32[]{:S(2)}) copy-start(f32[256]{0:T(256)} %param.13) | copy-start | bytes 3076
  20.5 145.9 %copy-start.8 = (bf16[3,3,3,8,4]{3,4,2,1,0:T(4,128)(2,1)S(1)}, bf16[3,3,3,8,4]{3,4,2,1,0:T(4,128)(2,1)}, u32[]{:S(2)}) copy-start(bf16[3,3,3,8,4]{3,4,2,1,0:T(4,128)(2,1)} %param.14) | copy-start | bytes 5188
  20.5 146.6 %copy-start.16 = (u32[256]{0:T(256)S(1)}, u32[256]{0:T(256)}, u32[]{:S(2)}) copy-start(u32[256]{0:T(256)} %constant.108) | copy-start | bytes 3076
  156.6 18.9 %copy-start.3 = (f32[1,2,8,5,256]{4,2,3,1,0:T(8,128)}, f32[1,2,8,5,256]{4,2,3,1,0:T(8,128)S(1)}, u32[]{:S(2)}) copy-start(f32[1,2,8,5,256]{4,2,3,1,0:T(8,128)S(1)} %get-tuple-element.280) | copy-start | bytes 245764
  157.9 17.3 %all-to-all-start = ((bf16[64,2,256]{2,1,0:T(2,128)(2,1)}), bf16[64,2,256]{2,1,0:T(2,128)(2,1)S(1)}, u32[]{:S(2)}, u32[]{:S(2)}) async-start(bf16[64,2,256]{2,1,0:T(2,128)(2,1)} %reshape.188), calls=%async_computation | async-start | bytes 131072 | tf_op jit(solution)/shard_map/all_to_all | solution.py:89
  182.6 25.9 %copy-start.12 = (f32[4]{0:T(128)S(1)}, f32[4]{0:T(128)}, u32[]{:S(2)}) copy-start(f32[4]{0:T(128)} %param.15) | copy-start | bytes 52
  182.6 25.9 %copy-start.14 = (f32[4]{0:T(128)S(1)}, f32[4]{0:T(128)}, u32[]{:S(2)}) copy-start(f32[4]{0:T(128)} %param.16) | copy-start | bytes 52
  182.6 26.7 %copy-start.7 = (bf16[1,4,64,2,32]{2,4,3,1,0:T(8,128)(2,1)S(1)}, bf16[1,4,64,2,32]{2,4,3,1,0:T(8,128)(2,1)}, u32[]{:S(2)}) copy-start(bf16[1,4,64,2,32]{2,4,3,1,0:T(8,128)(2,1)} %param.17) | copy-start | bytes 98308
  184.3 34.2 %copy-start.9 = (bf16[3,3,3,8,4]{3,4,2,1,0:T(4,128)(2,1)S(1)}, bf16[3,3,3,8,4]{3,4,2,1,0:T(4,128)(2,1)}, u32[]{:S(2)}) copy-start(bf16[3,3,3,8,4]{3,4,2,1,0:T(4,128)(2,1)} %rev.3) | copy-start | bytes 5188
  225.4 9.5 %copy-start.4 = (f32[1,2,8,5,256]{4,2,3,1,0:T(8,128)S(1)}, f32[1,2,8,5,256]{4,2,3,1,0:T(8,128)}, u32[]{:S(2)}) copy-start(f32[1,2,8,5,256]{4,2,3,1,0:T(8,128)} %copy-done.3) | copy-start | bytes 245764
  225.4 9.5 %copy-start.5 = (f32[1,2,8,5,256]{4,2,3,1,0:T(8,128)S(1)}, f32[1,2,8,5,256]{4,2,3,1,0:T(8,128)}, u32[]{:S(2)}) copy-start(f32[1,2,8,5,256]{4,2,3,1,0:T(8,128)} %get-tuple-element.279) | copy-start | bytes 245764
  229.3 14.9 %all-to-all-start.1 = ((f32[64,1,512]{2,1,0:T(1,128)}), f32[64,1,512]{2,1,0:T(1,128)S(1)}, u32[]{:S(2)}, u32[]{:S(2)}) async-start(f32[64,1,512]{2,1,0:T(1,128)} %reshape.190), calls=%async_computation.1 | async-start | bytes 262144 | tf_op jit(solution)/shard_map/all_to_all | solution.py:147
  234.8 280.5 %all-reduce.10.cloned.1.call-start = ((), (), s32[]{:S(2)}) async-start(), calls=%async_computation.2 | async-start | bytes 7077888
  245.7 76.3 %copy-start.2 = (bf16[1,3,4,64,128]{4,0,3,2,1:T(2,128)(2,1)S(1)}, bf16[1,3,4,64,128]{4,0,3,2,1:T(2,128)(2,1)}, u32[]{:S(2)}) copy-start(bf16[1,3,4,64,128]{4,0,3,2,1:T(2,128)(2,1)} %copy-done.1) | copy-start | bytes 589828
  324.9 0.7 copy-start.15
  324.9 5.4 copy-start.6
Sparse Core Ops, SparseCore 0:
  325.0 190.2 all-reduce.9
